TPU v7x, 256 devices: a whole 4x4x8 slice. The times are simulated.
256 devices in a mesh: section: 16 (over x_hi, y, core), tm: 16 (over z, x_lo).
Axes of the slice: x: 4 (x_hi: 2, x_lo: 2; x = x_hi * 2 + x_lo), y: 4, z: 8, core: 2. Of those that a mesh axis runs over, the one named last changes fastest.
Arguments:
- fwd_input: bfloat16 [16, 2048, 1536], P('section', 'tm'), may hold values from -6 to 6
- saved_input: bfloat16 [16, 2048, 1536], P('section', 'tm'), may hold values from -6 to 6
- grad_in: bfloat16 [16, 2048, 1536], P('section', 'tm'), may hold values from -6 to 6
- gain: float32 [16, 1536], P('section'), may hold values from 0.25 to 1.75
- kernel: float32 [16, 31, 1536], P('section'), may hold values from -1 to 1
- w_out: bfloat16 [16, 1536, 1536], P('section', 'tm'), may hold values from -0.15625 to 0.15625
- lengths: int32 [32], replicated, may hold values from 1 to 2048, 49152 in all
- plan: int32 [16, 2], P('section'), may hold values from 0 to 31
Outputs:
- passed_activation: bfloat16 [16, 2048, 1536], P('section', 'tm')
- passed_gradient: bfloat16 [16, 2048, 1536], P('section', 'tm')
- weight_grad: float32 [16, 1536, 1536], P('section', 'tm')
- kernel_grad: float32 [16, 31, 1536], P('section')
- gain_grad: float32 [16, 1536], P('section')
Inputs may be any that keep to these rules, and one draw needn't show every extreme that they name: `lengths`: 32 valid counts summing to 49152, the largest exactly 2048. `plan`: indices into lengths.
All inputs are finite; a program needn't handle non-finite values.
Results may differ from a plain program's by a relative error of at most 0.017.
Values may be sent and summed in bfloat16 or wider, within the bound.
No kernel may reach another device: no remote copies, remote signals or barrier semaphores. Data moves between devices by JAX's collectives and lax.ppermute only.
A program may use at most 64 MiB of HBM per device.

v0:
```python
import jax
import jax.numpy as jnp
from jax import lax
from jax.sharding import PartitionSpec as P

KW = 31


def extended(array, sides, width):
    for axis, dim in sides:
        size, length = (lax.axis_size(axis), array.shape[dim])
        up = [(i, (i + 1) % size) for i in range(size - 1)]
        down = [(j, i) for i, j in up]
        last = lax.slice_in_dim(array, length - width, length, axis=dim)
        first = lax.slice_in_dim(array, 0, width, axis=dim)
        before = lax.ppermute(last, axis, up)
        after = lax.ppermute(first, axis, down)
        array = jnp.concatenate([before, array, after], axis=dim)
    return array


def from_behind(array, axis, by):
    length = lax.axis_size(axis)
    pairs = [(i, i + by) for i in range(length) if 0 <= i + by < length]
    return lax.ppermute(array, axis, pairs)


def normalize(values):
    center = values - jnp.mean(values, axis=-1, keepdims=True)
    inverse = lax.rsqrt(jnp.mean(center * center, axis=-1, keepdims=True) + 1e-05)
    return (center * inverse, inverse)


def swish_act(values):
    return values * jax.nn.sigmoid(values)


def conv_taps(padded, kernel_rows, frames):
    running = jnp.zeros(padded.shape[:-2] + (frames, padded.shape[-1]), jnp.float32)
    for tap_index in range(KW):
        running = running + kernel_rows[tap_index] * padded[..., tap_index : tap_index + frames, :]
    return running


def per_device(fwd_input, saved_input, grad_in, gain, kernel, w_out, lengths, plan):
    frames = fwd_input.shape[1]
    pieces = lax.axis_size("tm")
    margin = KW // 2
    factor = float(frames * pieces) ** (-0.5)
    position = lax.axis_index("tm") * frames + lax.iota(jnp.int32, frames)
    slot_ids = lax.iota(jnp.int32, lengths.shape[0])
    fwd_len = jnp.sum(jnp.where(slot_ids == plan[0, 0], lengths, 0))
    bwd_len = jnp.sum(jnp.where(slot_ids == plan[0, 1], lengths, 0))
    fwd_mask = (position < fwd_len).astype(jnp.float32)[:, None]
    bwd_mask = (position < bwd_len).astype(jnp.float32)[:, None]
    gain_row = gain[0]
    kernel_rows = kernel[0]
    w_rows = w_out[0]
    upstream = grad_in[0]
    fwd_float = fwd_input[0].astype(jnp.float32)
    fwd_hat, unused_inverse = normalize(fwd_float)
    saved_hat, inverse = normalize(saved_input[0].astype(jnp.float32))
    conv_fwd = (fwd_hat * gain_row * fwd_mask).astype(jnp.bfloat16)
    conv_saved = (saved_hat * gain_row * bwd_mask).astype(jnp.bfloat16)
    padded = extended(jnp.stack([conv_fwd, conv_saved]), (("tm", 1),), margin)
    padded_float = padded.astype(jnp.float32)
    mixed_all = conv_taps(padded_float, kernel_rows, frames)
    mixed_saved = mixed_all[1]
    hidden_fwd = swish_act(mixed_all[0]).astype(jnp.bfloat16)
    hidden_saved = swish_act(mixed_saved).astype(jnp.bfloat16)
    columns = hidden_fwd
    product = jnp.dot(
        columns,
        lax.all_gather(w_rows, "tm", axis=0, tiled=True),
        preferred_element_type=jnp.float32,
    )
    hidden_grad = lax.dot_general(
        upstream,
        lax.all_gather(w_rows, "tm", axis=0, tiled=True),
        (((1,), (1,)), ((), ())),
        preferred_element_type=jnp.float32,
    )
    output = (fwd_float + product).astype(jnp.bfloat16)
    passed_activation = from_behind(output[None], "section", 1)
    gate_sig = jax.nn.sigmoid(mixed_saved)
    conv_grad = (hidden_grad * (gate_sig + mixed_saved * gate_sig * (1.0 - gate_sig))).astype(
        jnp.bfloat16
    )
    pad_grad = extended(conv_grad, (("tm", 0),), margin).astype(jnp.float32)
    input_grad = jnp.zeros((frames, conv_grad.shape[1]), jnp.float32)
    for tap_index in range(KW):
        begin_at = 2 * margin - tap_index
        input_grad = input_grad + kernel_rows[tap_index] * pad_grad[begin_at : begin_at + frames]
    grad_float = conv_grad.astype(jnp.float32)
    pad_saved = padded_float[1]
    kernel_local = (
        jnp.stack(
            [
                jnp.sum(grad_float * pad_saved[tap_index : tap_index + frames], axis=0)
                for tap_index in range(KW)
            ]
        )
        * factor
    )
    norm_grad = input_grad * bwd_mask
    gain_local = jnp.sum(norm_grad * saved_hat, axis=0) * factor
    kernel_grad, gain_grad = (
        lax.psum(kernel_local.astype(jnp.bfloat16), "tm").astype(jnp.float32),
        lax.psum(gain_local.astype(jnp.bfloat16), "tm").astype(jnp.float32),
    )
    columns = hidden_saved
    partial_value = (
        lax.dot_general(
            columns, upstream, (((0,), (0,)), ((), ())), preferred_element_type=jnp.float32
        )
        * factor
    )
    weight_grad = lax.psum_scatter(
        lax.optimization_barrier(partial_value.astype(jnp.bfloat16))
        .astype(jnp.float32)
        .astype(jnp.bfloat16),
        "tm",
        scatter_dimension=0,
        tiled=True,
    ).astype(jnp.float32)
    hat_grad = norm_grad * gain_row
    input_back = upstream.astype(jnp.float32) + inverse * (
        hat_grad
        - jnp.mean(hat_grad, axis=-1, keepdims=True)
        - saved_hat * jnp.mean(hat_grad * saved_hat, axis=-1, keepdims=True)
    )
    passed_gradient = from_behind(input_back.astype(jnp.bfloat16)[None], "section", -1)
    return (
        passed_activation,
        passed_gradient,
        weight_grad[None],
        kernel_grad[None],
        gain_grad[None],
    )


def solution(mesh):
    placed = (
        P("section", "tm", None),
        P("section", "tm", None),
        P("section", "tm", None),
        P("section", None),
        P("section", None, None),
        P("section", "tm", None),
        P(),
        P("section", None),
    )
    return jax.shard_map(
        per_device,
        mesh=mesh,
        in_specs=placed,
        out_specs=(
            P("section", "tm", None),
            P("section", "tm", None),
            P("section", "tm", None),
            P("section", None, None),
            P("section", None),
        ),
        check_vma=False,
    )
```

profile of v0, /device:TPU:42, one launch (start us, length us, event | category | flops | bytes accessed | tf_op | source)
XLA Modules:
  0.0 398.9 jit_solution(7578486727265539355)
XLA Ops:
  7.2 0.0 copy-start.1
  7.2 0.0 copy-start
  7.2 0.0 all-gather.3.cloned.1.call-start
  7.2 0.7 all-gather.3.cloned.1.call-update
  7.9 0.0 all-reduce.2.cloned.1.call-start
  8.0 0.7 reduce.3
  8.7 1.3 fusion.152
  10.0 2.6 fusion.146
  12.6 1.3 compare_convert_fusion
  13.9 0.0 copy-start.69
  13.9 1.1 convert_reduce_fusion.1
  15.0 1.1 convert_reduce_fusion
  16.2 1.2 fusion.52
  17.5 0.3 fusion.73
  17.7 0.4 fusion.56
  18.2 3.8 collective-permute-start
  22.0 2.0 collective-permute-start.1
  24.1 0.3 slice_reduce_fusion.30
  24.6 0.2 slice_reduce_fusion.29
  24.9 0.0 copy-start.61
  24.9 0.0 copy-start.63
  24.9 0.6 collective-permute-done
  25.5 6.0 %collective-permute-done.1 = bf16[2,15,1536]{2,1,0:T(8,128)(2,1)S(1)} collective-permute-done((bf16[2,15,1536]{2,1,0:T(8,128)(2,1)S(1)}, bf16[2,15,1536]{2,1,0:T(8,128)(2,1)S(1)}, u32[]{:S(2)}, u32[]{:S(2)}) %collective-permute-start.1) | collective-permute-done | bytes 92192 | tf_op jit(solution)/shard_map/ppermute | solution.py:17
  31.5 0.3 maximum_convert_fusion
  32.1 0.0 copy-start.3
  32.1 6.8 %fusion.20 = f32[2,128,1536]{2,1,0:T(8,128)} fusion(f32[2,158,1536]{2,1,0:T(8,128)S(1)} %maximum_convert_fusion, f32[1536]{0:T(1024)S(1)} %get-tuple-element.68, f32[1536]{0:T(1024)S(1)} %get-tuple-element.69, f32[1536]{0:T(1024)S(1)} %get-tuple-element.40, f32[1536]{0:T(1024)S(1)} %get-tuple-element.41, f32[1536]{0:T(1024)S(1)} %get-tuple-element.42, ...), kind=kLoop, calls=%fused_computation.43 | loop fusion | flops 23986176 | bytes 50522112 | tf_op jit(solution)/shard_map/add | solution.py:41
  38.9 86.8 %all-gather.3.cloned.1.call-done = bf16[1,1536,1536]{2,1,0:T(8,128)(2,1)} async-done(((bf16[1,96,1536]{2,1,0:T(8,128)(2,1)}), bf16[1,1536,1536]{2,1,0:T(8,128)(2,1)}) %all-gather.3.cloned.1.call-update) | async-done | bytes 4718608 | tf_op jit(solution)/shard_map/all_gather | solution.py:74
  125.8 5.5 %fusion.103 = (f32[1536]{0:T(1024)S(1)}, f32[1536]{0:T(1024)S(1)}, f32[1536]{0:T(1024)S(1)}, f32[1536]{0:T(1024)S(1)}, f32[1536]{0:T(1024)S(1)}, /*index=5*/f32[...) fusion(f32[2,158,1536]{2,1,0:T(8,128)S(1)} %maximum_convert_fus, ...), kind=kOutput, calls=%fused_computation.163 | convolution fusion | flops 611037696 | bytes 16594944 | tf_op jit(solution)/shard_map/dot_general | solution.py:77
  131.2 2.0 fusion.104
  133.6 0.6 stack.113
  134.2 0.6 stack.114
  134.8 0.6 stack.115
  135.4 0.6 stack.116
  136.0 0.6 stack.117
  136.6 0.6 stack.118
  137.2 0.6 stack.119
  137.8 1.8 stack.133
  139.6 0.8 broadcast_in_dim.42
  140.3 0.0 all-reduce.2.cloned.1.call-update
  140.4 0.0 reduce-scatter.2.cloned.1.call-start
  140.4 3.6 fusion
  144.0 0.0 reduce-scatter.2.cloned.1.call-update
  144.1 2.4 collective-permute-start.3
  146.8 0.0 copy-start.62
  146.8 0.0 copy-start.64
  146.9 3.5 collective-permute-start.4
  150.4 3.9 fusion.17
  154.3 2.1 collective-permute-start.2
  156.4 0.0 collective-permute-done.3
  156.4 0.0 collective-permute-done.4
  156.4 0.1 maximum_convert_fusion.1
  156.9 5.1 %fusion.72 = (f32[1536]{0:T(1024)S(1)}, f32[128]{0:T(128)S(1)}, f32[128]{0:T(128)S(1)}, f32[128,1536]{1,0:T(8,128)S(1)}) fusion(bf16[1,128,1536]{2,1,0:T(8,128)(2,1)S(1)} %copy-done, f32[128]{0:T(128)S(1)} %copy-done.68, f32[128]{0:T(128)S(1)} %copy-done.66, f32[1536]{0:T(1024)S(1)} %reduce.3, f32[128]{0:T(128)S(1)} %copy-done.70, ...), kind=kLoop, calls=%fused_computation.132 | loop fusion | flops 13957376 | bytes 25764352 | tf_op jit(solution)/shard_map/reduce_sum | solution.py:106
  162.0 0.4 fusion.141
  162.4 3.6 collective-permute-start.5
  166.1 31.3 %psum.15 = bf16[1,1536]{1,0:T(2,128)(2,1)S(1)} all-reduce(bf16[1,1536]{1,0:T(2,128)(2,1)S(1)} %broadcast_in_dim.44), channel_id=1, replica_groups=mesh['section'=16,'tm'=16] {'tm'}, use_global_device_ids=true, to_apply=%region_42.43 | all-reduce | flops 1536 | bytes 6144 | tf_op jit(solution)/shard_map/psum | solution.py:109
  197.4 0.6 broadcast_in_dim.45
  198.0 78.2 %all-reduce.2.cloned.1.call-done = bf16[1,31,1536]{2,0,1:T(2,128)(2,1)} async-done(((bf16[1,31,1536]{2,0,1:T(2,128)(2,1)}), bf16[1,31,1536]{2,0,1:T(2,128)(2,1)}) %all-reduce.2.cloned.1.call-update) | async-done | bytes 95248 | tf_op jit(solution)/shard_map/psum | solution.py:108
  276.2 1.8 broadcast_in_dim.43
  278.0 0.0 collective-permute-done.2
  278.0 0.0 collective-permute-done.5
  278.0 111.0 %reduce-scatter.2.cloned.1.call-done = bf16[96,1536]{1,0:T(8,128)(2,1)} async-done(((bf16[1536,1536]{1,0:T(8,128)(2,1)}), bf16[96,1536]{1,0:T(8,128)(2,1)}) %reduce-scatter.2.cloned.1.call-update) | async-done | bytes 294928 | tf_op jit(solution)/shard_map/reduce_scatter | solution.py:118
  389.0 1.8 bitcast_convert_fusion
  390.9 0.7 copy.16
  391.6 0.7 copy.17
  (168 shorter events, 0.5 us)
Async XLA Ops:
  7.2 10.6 %copy-start.1 = (bf16[1,128,1536]{2,1,0:T(8,128)(2,1)S(1)}, bf16[1,128,1536]{2,1,0:T(8,128)(2,1)}, u32[]{:S(2)}) copy-start(bf16[1,128,1536]{2,1,0:T(8,128)(2,1)} %param.8) | copy-start | bytes 1179652
  7.2 10.3 %copy-start = (bf16[1,128,1536]{2,1,0:T(8,128)(2,1)S(1)}, bf16[1,128,1536]{2,1,0:T(8,128)(2,1)}, u32[]{:S(2)}) copy-start(bf16[1,128,1536]{2,1,0:T(8,128)(2,1)} %param.9) | copy-start | bytes 1179652
  7.2 118.6 %all-gather.3.cloned.1.call-start = ((), (), s32[]{:S(2)}) async-start(), calls=%async_computation.3 | async-start | bytes 5013504 | tf_op jit(solution)/shard_map/all_gather | solution.py:74
  7.9 268.3 %all-reduce.2.cloned.1.call-start = ((), (), s32[]{:S(2)}) async-start(), calls=%async_computation.2 | async-start | bytes 380928 | tf_op jit(solution)/shard_map/psum | solution.py:108
  17.7 7.8 %copy-start.67 = (f32[128]{0:T(128)}, f32[128]{0:T(128)S(1)}, u32[]{:S(2)}) copy-start(f32[128]{0:T(128)S(1)} %get-tuple-element.84) | copy-start | bytes 1540
  18.2 7.3 %collective-permute-start = (bf16[2,15,1536]{2,1,0:T(8,128)(2,1)S(1)}, bf16[2,15,1536]{2,1,0:T(8,128)(2,1)S(1)}, u32[]{:S(2)}, u32[]{:S(2)}) collective-permute-start(bf16[2,15,1536]{2,1,0:T(8,128)(2,1)S(1)} %get-tuple-element.73), channel_id=1, source_target_pairs={{0,1},{1,2},{2,3},{3,4},{4,5},{5,6},{6,7},{7,8},{8,9},{9,10},{10,1... | collective-permute-start | bytes 276488 | tf_op jit(solution)/shard_map/ppermute | solution.py:16
  22.0 9.5 %collective-permute-start.1 = (bf16[2,15,1536]{2,1,0:T(8,128)(2,1)S(1)}, bf16[2,15,1536]{2,1,0:T(8,128)(2,1)S(1)}, u32[]{:S(2)}, u32[]{:S(2)}) collective-permute-start(bf16[2,15,1536]{2,1,0:T(8,128)(2,1)S(1)} %get-tuple-element.74), channel_id=1, source_target_pairs={{1,0},{2,1},{3,2},{4,3},{5,4},{6,5},{7,6},{8,7},{9,8},{10,9},{11,1... | collective-permute-start | bytes 276488 | tf_op jit(solution)/shard_map/ppermute | solution.py:17
  24.4 7.4 %copy-start.5 = (f32[1536]{0:T(1024)}, f32[1536]{0:T(1024)S(1)}, u32[]{:S(2)}) copy-start(f32[1536]{0:T(1024)S(1)} %get-tuple-element.40) | copy-start | bytes 18436
  24.4 7.4 %copy-start.7 = (f32[1536]{0:T(1024)}, f32[1536]{0:T(1024)S(1)}, u32[]{:S(2)}) copy-start(f32[1536]{0:T(1024)S(1)} %get-tuple-element.41) | copy-start | bytes 18436
  24.4 7.4 %copy-start.9 = (f32[1536]{0:T(1024)}, f32[1536]{0:T(1024)S(1)}, u32[]{:S(2)}) copy-start(f32[1536]{0:T(1024)S(1)} %get-tuple-element.42) | copy-start | bytes 18436
  24.4 7.4 %copy-start.11 = (f32[1536]{0:T(1024)}, f32[1536]{0:T(1024)S(1)}, u32[]{:S(2)}) copy-start(f32[1536]{0:T(1024)S(1)} %get-tuple-element.43) | copy-start | bytes 18436
  24.4 7.4 %copy-start.13 = (f32[1536]{0:T(1024)}, f32[1536]{0:T(1024)S(1)}, u32[]{:S(2)}) copy-start(f32[1536]{0:T(1024)S(1)} %get-tuple-element.44) | copy-start | bytes 18436
  24.4 7.4 %copy-start.15 = (f32[1536]{0:T(1024)}, f32[1536]{0:T(1024)S(1)}, u32[]{:S(2)}) copy-start(f32[1536]{0:T(1024)S(1)} %get-tuple-element.45) | copy-start | bytes 18436
  24.4 7.4 %copy-start.17 = (f32[1536]{0:T(1024)}, f32[1536]{0:T(1024)S(1)}, u32[]{:S(2)}) copy-start(f32[1536]{0:T(1024)S(1)} %get-tuple-element.46) | copy-start | bytes 18436
  24.4 7.4 %copy-start.19 = (f32[1536]{0:T(1024)}, f32[1536]{0:T(1024)S(1)}, u32[]{:S(2)}) copy-start(f32[1536]{0:T(1024)S(1)} %get-tuple-element.47) | copy-start | bytes 18436
  24.5 7.4 %copy-start.21 = (f32[1536]{0:T(1024)}, f32[1536]{0:T(1024)S(1)}, u32[]{:S(2)}) copy-start(f32[1536]{0:T(1024)S(1)} %get-tuple-element.48) | copy-start | bytes 18436
  24.5 7.4 %copy-start.23 = (f32[1536]{0:T(1024)}, f32[1536]{0:T(1024)S(1)}, u32[]{:S(2)}) copy-start(f32[1536]{0:T(1024)S(1)} %get-tuple-element.49) | copy-start | bytes 18436
  24.5 7.4 %copy-start.25 = (f32[1536]{0:T(1024)}, f32[1536]{0:T(1024)S(1)}, u32[]{:S(2)}) copy-start(f32[1536]{0:T(1024)S(1)} %get-tuple-element.50) | copy-start | bytes 18436
  24.5 7.4 %copy-start.27 = (f32[1536]{0:T(1024)}, f32[1536]{0:T(1024)S(1)}, u32[]{:S(2)}) copy-start(f32[1536]{0:T(1024)S(1)} %get-tuple-element.51) | copy-start | bytes 18436
  24.5 7.4 %copy-start.29 = (f32[1536]{0:T(1024)}, f32[1536]{0:T(1024)S(1)}, u32[]{:S(2)}) copy-start(f32[1536]{0:T(1024)S(1)} %get-tuple-element.52) | copy-start | bytes 18436
  24.5 7.4 %copy-start.31 = (f32[1536]{0:T(1024)}, f32[1536]{0:T(1024)S(1)}, u32[]{:S(2)}) copy-start(f32[1536]{0:T(1024)S(1)} %get-tuple-element.53) | copy-start | bytes 18436
  24.5 7.4 %copy-start.33 = (f32[1536]{0:T(1024)}, f32[1536]{0:T(1024)S(1)}, u32[]{:S(2)}) copy-start(f32[1536]{0:T(1024)S(1)} %get-tuple-element.54) | copy-start | bytes 18436
  24.5 7.4 %copy-start.35 = (f32[1536]{0:T(1024)}, f32[1536]{0:T(1024)S(1)}, u32[]{:S(2)}) copy-start(f32[1536]{0:T(1024)S(1)} %get-tuple-element.55) | copy-start | bytes 18436
  24.5 7.4 %copy-start.37 = (f32[1536]{0:T(1024)}, f32[1536]{0:T(1024)S(1)}, u32[]{:S(2)}) copy-start(f32[1536]{0:T(1024)S(1)} %get-tuple-element.56) | copy-start | bytes 18436
  24.5 7.4 %copy-start.39 = (f32[1536]{0:T(1024)}, f32[1536]{0:T(1024)S(1)}, u32[]{:S(2)}) copy-start(f32[1536]{0:T(1024)S(1)} %get-tuple-element.57) | copy-start | bytes 18436
  32.1 93.7 %copy-start.3 = (bf16[1,128,1536]{2,1,0:T(8,128)(2,1)S(1)}, bf16[1,128,1536]{2,1,0:T(8,128)(2,1)}, u32[]{:S(2)}) copy-start(bf16[1,128,1536]{2,1,0:T(8,128)(2,1)} %param.10) | copy-start | bytes 1179652
  140.4 248.7 %reduce-scatter.2.cloned.1.call-start = ((), (), s32[]{:S(2)}) async-start(), calls=%async_computation.1 | async-start | bytes 5013504 | tf_op jit(solution)/shard_map/reduce_scatter | solution.py:118
  144.1 12.3 %collective-permute-start.3 = (bf16[15,1536]{1,0:T(8,128)(2,1)S(1)}, bf16[15,1536]{1,0:T(8,128)(2,1)S(1)}, u32[]{:S(2)}, u32[]{:S(2)}) collective-permute-start(bf16[15,1536]{1,0:T(8,128)(2,1)S(1)} %get-tuple-element.75), channel_id=1, source_target_pairs={{0,1},{1,2},{2,3},{3,4},{4,5},{5,6},{6,7},{7,8},{8,9},{9,10},{10,1... | collective-permute-start | bytes 138248 | tf_op jit(solution)/shard_map/ppermute | solution.py:16
  146.5 10.0 %copy-start.6 = (f32[1536]{0:T(1024)S(1)}, f32[1536]{0:T(1024)}, u32[]{:S(2)}) copy-start(f32[1536]{0:T(1024)} %copy-done.5) | copy-start | bytes 18436
  146.5 10.0 %copy-start.8 = (f32[1536]{0:T(1024)S(1)}, f32[1536]{0:T(1024)}, u32[]{:S(2)}) copy-start(f32[1536]{0:T(1024)} %copy-done.7) | copy-start | bytes 18436
  146.6 10.0 %copy-start.10 = (f32[1536]{0:T(1024)S(1)}, f32[1536]{0:T(1024)}, u32[]{:S(2)}) copy-start(f32[1536]{0:T(1024)} %copy-done.9) | copy-start | bytes 18436
  146.6 10.0 %copy-start.12 = (f32[1536]{0:T(1024)S(1)}, f32[1536]{0:T(1024)}, u32[]{:S(2)}) copy-start(f32[1536]{0:T(1024)} %copy-done.11) | copy-start | bytes 18436
  146.6 10.0 %copy-start.14 = (f32[1536]{0:T(1024)S(1)}, f32[1536]{0:T(1024)}, u32[]{:S(2)}) copy-start(f32[1536]{0:T(1024)} %copy-done.13) | copy-start | bytes 18436
  146.6 10.0 %copy-start.16 = (f32[1536]{0:T(1024)S(1)}, f32[1536]{0:T(1024)}, u32[]{:S(2)}) copy-start(f32[1536]{0:T(1024)} %copy-done.15) | copy-start | bytes 18436
  146.6 10.0 %copy-start.18 = (f32[1536]{0:T(1024)S(1)}, f32[1536]{0:T(1024)}, u32[]{:S(2)}) copy-start(f32[1536]{0:T(1024)} %copy-done.17) | copy-start | bytes 18436
  146.6 10.0 %copy-start.20 = (f32[1536]{0:T(1024)S(1)}, f32[1536]{0:T(1024)}, u32[]{:S(2)}) copy-start(f32[1536]{0:T(1024)} %copy-done.19) | copy-start | bytes 18436
  146.6 10.0 %copy-start.22 = (f32[1536]{0:T(1024)S(1)}, f32[1536]{0:T(1024)}, u32[]{:S(2)}) copy-start(f32[1536]{0:T(1024)} %copy-done.21) | copy-start | bytes 18436
  146.6 10.0 %copy-start.24 = (f32[1536]{0:T(1024)S(1)}, f32[1536]{0:T(1024)}, u32[]{:S(2)}) copy-start(f32[1536]{0:T(1024)} %copy-done.23) | copy-start | bytes 18436
  146.6 10.0 %copy-start.26 = (f32[1536]{0:T(1024)S(1)}, f32[1536]{0:T(1024)}, u32[]{:S(2)}) copy-start(f32[1536]{0:T(1024)} %copy-done.25) | copy-start | bytes 18436
  146.6 10.0 %copy-start.28 = (f32[1536]{0:T(1024)S(1)}, f32[1536]{0:T(1024)}, u32[]{:S(2)}) copy-start(f32[1536]{0:T(1024)} %copy-done.27) | copy-start | bytes 18436
  146.7 10.0 %copy-start.30 = (f32[1536]{0:T(1024)S(1)}, f32[1536]{0:T(1024)}, u32[]{:S(2)}) copy-start(f32[1536]{0:T(1024)} %copy-done.29) | copy-start | bytes 18436
  146.7 10.0 %copy-start.32 = (f32[1536]{0:T(1024)S(1)}, f32[1536]{0:T(1024)}, u32[]{:S(2)}) copy-start(f32[1536]{0:T(1024)} %copy-done.31) | copy-start | bytes 18436
  146.7 10.0 %copy-start.34 = (f32[1536]{0:T(1024)S(1)}, f32[1536]{0:T(1024)}, u32[]{:S(2)}) copy-start(f32[1536]{0:T(1024)} %copy-done.33) | copy-start | bytes 18436
  146.7 10.0 %copy-start.36 = (f32[1536]{0:T(1024)S(1)}, f32[1536]{0:T(1024)}, u32[]{:S(2)}) copy-start(f32[1536]{0:T(1024)} %copy-done.35) | copy-start | bytes 18436
  146.7 10.0 %copy-start.38 = (f32[1536]{0:T(1024)S(1)}, f32[1536]{0:T(1024)}, u32[]{:S(2)}) copy-start(f32[1536]{0:T(1024)} %copy-done.37) | copy-start | bytes 18436
  146.7 10.0 %copy-start.40 = (f32[1536]{0:T(1024)S(1)}, f32[1536]{0:T(1024)}, u32[]{:S(2)}) copy-start(f32[1536]{0:T(1024)} %copy-done.39) | copy-start | bytes 18436
  146.7 10.0 %copy-start.42 = (f32[1536]{0:T(1024)S(1)}, f32[1536]{0:T(1024)}, u32[]{:S(2)}) copy-start(f32[1536]{0:T(1024)} %copy-done.41) | copy-start | bytes 18436
  146.7 10.0 %copy-start.44 = (f32[1536]{0:T(1024)S(1)}, f32[1536]{0:T(1024)}, u32[]{:S(2)}) copy-start(f32[1536]{0:T(1024)} %copy-done.43) | copy-start | bytes 18436
  146.7 10.0 %copy-start.46 = (f32[1536]{0:T(1024)S(1)}, f32[1536]{0:T(1024)}, u32[]{:S(2)}) copy-start(f32[1536]{0:T(1024)} %copy-done.45) | copy-start | bytes 18436
  146.7 10.0 %copy-start.48 = (f32[1536]{0:T(1024)S(1)}, f32[1536]{0:T(1024)}, u32[]{:S(2)}) copy-start(f32[1536]{0:T(1024)} %copy-done.47) | copy-start | bytes 18436
  146.8 10.0 %copy-start.50 = (f32[1536]{0:T(1024)S(1)}, f32[1536]{0:T(1024)}, u32[]{:S(2)}) copy-start(f32[1536]{0:T(1024)} %copy-done.49) | copy-start | bytes 18436
  146.8 10.0 %copy-start.52 = (f32[1536]{0:T(1024)S(1)}, f32[1536]{0:T(1024)}, u32[]{:S(2)}) copy-start(f32[1536]{0:T(1024)} %copy-done.51) | copy-start | bytes 18436
  146.8 10.0 %copy-start.54 = (f32[1536]{0:T(1024)S(1)}, f32[1536]{0:T(1024)}, u32[]{:S(2)}) copy-start(f32[1536]{0:T(1024)} %copy-done.53) | copy-start | bytes 18436
  146.8 10.0 %copy-start.56 = (f32[1536]{0:T(1024)S(1)}, f32[1536]{0:T(1024)}, u32[]{:S(2)}) copy-start(f32[1536]{0:T(1024)} %copy-done.55) | copy-start | bytes 18436
  146.8 10.0 %copy-start.58 = (f32[1536]{0:T(1024)S(1)}, f32[1536]{0:T(1024)}, u32[]{:S(2)}) copy-start(f32[1536]{0:T(1024)} %copy-done.57) | copy-start | bytes 18436
  146.8 10.0 %copy-start.60 = (f32[1536]{0:T(1024)S(1)}, f32[1536]{0:T(1024)}, u32[]{:S(2)}) copy-start(f32[1536]{0:T(1024)} %copy-done.59) | copy-start | bytes 18436
  146.8 10.0 %copy-start.62 = (f32[1536]{0:T(1024)S(1)}, f32[1536]{0:T(1024)}, u32[]{:S(2)}) copy-start(f32[1536]{0:T(1024)} %copy-done.61) | copy-start | bytes 18436
  146.8 10.0 %copy-start.64 = (f32[1536]{0:T(1024)S(1)}, f32[1536]{0:T(1024)}, u32[]{:S(2)}) copy-start(f32[1536]{0:T(1024)} %copy-done.63) | copy-start | bytes 18436
  146.8 10.0 %copy-start.66 = (f32[128]{0:T(128)S(1)}, f32[128]{0:T(128)}, u32[]{:S(2)}) copy-start(f32[128]{0:T(128)} %copy-done.65) | copy-start | bytes 1540
  146.8 10.0 %copy-start.68 = (f32[128]{0:T(128)S(1)}, f32[128]{0:T(128)}, u32[]{:S(2)}) copy-start(f32[128]{0:T(128)} %copy-done.67) | copy-start | bytes 1540
  146.9 10.0 %copy-start.70 = (f32[128]{0:T(128)S(1)}, f32[128]{0:T(128)}, u32[]{:S(2)}) copy-start(f32[128]{0:T(128)} %copy-done.69) | copy-start | bytes 1540
  146.9 9.6 %collective-permute-start.4 = (bf16[15,1536]{1,0:T(8,128)(2,1)S(1)}, bf16[15,1536]{1,0:T(8,128)(2,1)S(1)}, u32[]{:S(2)}, u32[]{:S(2)}) collective-permute-start(bf16[15,1536]{1,0:T(8,128)(2,1)S(1)} %get-tuple-element.76), channel_id=1, source_target_pairs={{1,0},{2,1},{3,2},{4,3},{5,4},{6,5},{7,6},{8,7},{9,8},{10,9},{11,1... | collective-permute-start | bytes 138248 | tf_op jit(solution)/shard_map/ppermute | solution.py:17
  154.3 123.7 %collective-permute-start.2 = (bf16[1,128,1536]{2,1,0:T(8,128)(2,1)}, bf16[1,128,1536]{2,1,0:T(8,128)(2,1)S(1)}, u32[]{:S(2)}, u32[]{:S(2)}) collective-permute-start(bf16[1,128,1536]{2,1,0:T(8,128)(2,1)} %fusion.17), channel_id=1, source_target_pairs={{0,16},{16,32},{32,48},{48,64},{64,80},{80,96},{96,112},{112,128},... | collective-permute-start | bytes 1179656 | tf_op jit(solution)/shard_map/ppermute | solution.py:25
  162.4 115.6 %collective-permute-start.5 = (bf16[1,128,1536]{2,1,0:T(8,128)(2,1)S(1)}, bf16[1,128,1536]{2,1,0:T(8,128)(2,1)S(1)}, u32[]{:S(2)}, u32[]{:S(2)}) collective-permute-start(bf16[1,128,1536]{2,1,0:T(8,128)(2,1)S(1)} %fusion.141), channel_id=1, source_target_pairs={{16,0},{32,16},{48,32},{64,48},{80,64},{96,80},{112,96},{128,112},... | collective-permute-start | bytes 1179656 | tf_op jit(solution)/shard_map/ppermute | solution.py:25
  (16 other events, 111.3 us)
Sparse Core Ops, SparseCore 0:
  9.8 115.9 all-gather.2
  140.5 135.6 all-reduce.1
  278.8 110.2 reduce-scatter.1
where the time goes:
time: 400 us; the launch traced here: 399 us
  waiting for transfers between devices  283 us (71%)
  blocking collectives  31.3 us (8%)
  other arithmetic  27.8 us (7%)
  starting transfers between devices  17.7 us (4%)
  between operations  15.3 us (4%)
  matrix products  13 us (3%)
  local copies, waits for them, and re-layouts  10.5 us (3%)
    reduce_scatter x1, waiting for transfers between devices, per_device(): lax.psum_scatter(lax.optimization_barrier(partial_value.astype(jnp.bfloat...  111 us
    all_gather x1, waiting for transfers between devices, per_device(): lax.all_gather(w_rows, 'tm', axis=0, tiled=True)  86.8 us
    psum x1, waiting for transfers between devices, per_device(): lax.psum(kernel_local.astype(jnp.bfloat16), 'tm').astype(jnp.float32)  78.2 us
    psum x1, blocking collectives, per_device(): lax.psum(gain_local.astype(jnp.bfloat16), 'tm').astype(jnp.float32)  31.3 us
  transfers between devices with their start and end apart: 9, of which 5 were waited for; matrix products, arithmetic and copies ran while one was open for 8% of the time, Pallas kernels for 0%

commit v1 on v0

--- a/solution.py
+++ b/solution.py
@@ -4,6 +4,11 @@
 from jax.sharding import PartitionSpec as P
 
 KW = 31
+
+
+def all_by_exchange(x, name, dim):
+    outgoing = jnp.stack([x] * lax.axis_size(name))
+    return jnp.concatenate(lax.all_to_all(outgoing, name, 0, 0), axis=dim)
 
 
 def extended(array, sides, width):
@@ -69,11 +74,7 @@
     hidden_fwd = swish_act(mixed_all[0]).astype(jnp.bfloat16)
     hidden_saved = swish_act(mixed_saved).astype(jnp.bfloat16)
     columns = hidden_fwd
-    product = jnp.dot(
-        columns,
-        lax.all_gather(w_rows, "tm", axis=0, tiled=True),
-        preferred_element_type=jnp.float32,
-    )
+    product = jnp.dot(columns, all_by_exchange(w_rows, "tm", 0), preferred_element_type=jnp.float32)
     hidden_grad = lax.dot_general(
         upstream,
         lax.all_gather(w_rows, "tm", axis=0, tiled=True),

time: 400 us -> 477 us (1.19)
  waiting for transfers between devices: 283 us -> 350 us
  starting transfers between devices: 17.7 us -> 29.1 us
    ppermute x2, waiting for transfers between devices: 5.99 us -> 121 us  [extended(): after = lax.ppermute(first, axis, down)]
    all_gather x1, waiting for transfers between devices: 86.8 us -> 29.4 us  [per_device(): lax.all_gather(w_rows, 'tm', axis=0, tiled=True)]
    all_to_all x0 -> x1, starting transfers between devices: none -> 9.63 us  [all_by_exchange(): return jnp.concatenate(lax.all_to_all(outgoing, name, 0, 0), axis=dim)]
    ppermute x2, waiting for transfers between devices: 0.62 us -> 9.4 us  [extended(): before = lax.ppermute(last, axis, up)]
  transfers between devices with their start and end apart: 9 -> 10, of which waited for: 5 -> 5; matrix products, arithmetic and copies ran while one was open for 8% -> 10% of each run, Pallas kernels for 0% -> 0%
where the time goes in v1:
time: 477 us; the launch traced here: 476 us
  waiting for transfers between devices  350 us (73%)
  blocking collectives  31.5 us (7%)
  starting transfers between devices  29.1 us (6%)
  other arithmetic  23.4 us (5%)
  between operations  15.2 us (3%)
  local copies, waits for them, and re-layouts  14.1 us (3%)
  matrix products  13.1 us (3%)
    ppermute x2, waiting for transfers between devices, extended(): after = lax.ppermute(first, axis, down)  121 us
    reduce_scatter x1, waiting for transfers between devices, per_device(): lax.psum_scatter(lax.optimization_barrier(partial_value.astype(jnp.bfloat...  111 us
    psum x1, waiting for transfers between devices, per_device(): lax.psum(kernel_local.astype(jnp.bfloat16), 'tm').astype(jnp.float32)  78.6 us
    psum x1, blocking collectives, per_device(): lax.psum(gain_local.astype(jnp.bfloat16), 'tm').astype(jnp.float32)  31.5 us
    all_gather x1, waiting for transfers between devices, per_device(): lax.all_gather(w_rows, 'tm', axis=0, tiled=True)  29.4 us
    all_to_all x1, starting transfers between devices, all_by_exchange(): return jnp.concatenate(lax.all_to_all(outgoing, name, 0, 0), axis=dim)  9.63 us
  transfers between devices with their start and end apart: 10, of which 5 were waited for; matrix products, arithmetic and copies ran while one was open for 10% of the time, Pallas kernels for 0%

profile of v1, /device:TPU:42, one launch (start us, length us, event | category | flops | bytes accessed | tf_op | source)
XLA Modules:
  0.0 476.2 jit_solution(6674409074623461309)
XLA Ops:
  7.2 0.0 all-gather.3.cloned.1.call-start
  7.2 0.7 all-gather.3.cloned.1.call-update
  7.9 3.6 stack.105
  11.5 0.0 copy-start.1
  11.5 9.6 %all-to-all-start = ((bf16[16,96,1536]{2,1,0:T(8,128)(2,1)}), bf16[16,96,1536]{2,1,0:T(8,128)(2,1)}, u32[]{:S(2)}, u32[]{:S(2)}) async-start(bf16[16,96,1536]{2,1,0:T(8,128)(2,1)} %stack.105), calls=%async_computation | async-start | bytes 9437184 | tf_op jit(solution)/shard_map/all_to_all | solution.py:11
  21.1 0.0 all-reduce.2.cloned.1.call-start
  21.2 0.6 fusion.143
  21.8 1.9 fusion.137
  23.8 1.3 compare_convert_fusion
  25.1 0.1 convert_reduce_fusion
  25.2 0.1 convert_reduce_fusion.1
  25.4 0.3 fusion.64
  25.6 0.3 fusion.43
  25.9 0.4 fusion.47
  26.3 0.1 copy-done.67
  26.4 2.5 collective-permute-start.1
  28.9 4.3 collective-permute-start
  33.2 0.3 slice_reduce_fusion.30
  33.7 0.2 slice_reduce_fusion.29
  34.0 0.0 copy-start.61
  34.0 120.7 %collective-permute-done.1 = bf16[2,15,1536]{2,1,0:T(8,128)(2,1)S(1)} collective-permute-done((bf16[2,15,1536]{2,1,0:T(8,128)(2,1)S(1)}, bf16[2,15,1536]{2,1,0:T(8,128)(2,1)S(1)}, u32[]{:S(2)}, u32[]{:S(2)}) %collective-permute-start.1) | collective-permute-done | bytes 92192 | tf_op jit(solution)/shard_map/ppermute | solution.py:22
  154.7 9.4 %collective-permute-done = bf16[2,15,1536]{2,1,0:T(8,128)(2,1)S(1)} collective-permute-done((bf16[2,15,1536]{2,1,0:T(8,128)(2,1)S(1)}, bf16[2,15,1536]{2,1,0:T(8,128)(2,1)S(1)}, u32[]{:S(2)}, u32[]{:S(2)}) %collective-permute-start) | collective-permute-done | bytes 92192 | tf_op jit(solution)/shard_map/ppermute | solution.py:21
  164.1 0.3 maximum_convert_fusion
  164.5 0.0 copy-start.3
  164.6 6.8 %fusion.11 = f32[2,128,1536]{2,1,0:T(8,128)} fusion(f32[2,158,1536]{2,1,0:T(8,128)S(1)} %maximum_convert_fusion, f32[1536]{0:T(1024)S(1)} %get-tuple-element.68, f32[1536]{0:T(1024)S(1)} %get-tuple-element.69, f32[1536]{0:T(1024)S(1)} %get-tuple-element.40, f32[1536]{0:T(1024)S(1)} %get-tuple-element.41, f32[1536]{0:T(1024)S(1)} %get-tuple-element.42, ...), kind=kLoop, calls=%fused_computation.41 | loop fusion | flops 23986176 | bytes 50522112 | tf_op jit(solution)/shard_map/add | solution.py:46
  171.5 29.4 %all-gather.3.cloned.1.call-done = bf16[1,1536,1536]{2,1,0:T(8,128)(2,1)} async-done(((bf16[1,96,1536]{2,1,0:T(8,128)(2,1)}), bf16[1,1536,1536]{2,1,0:T(8,128)(2,1)}) %all-gather.3.cloned.1.call-update) | async-done | bytes 4718608 | tf_op jit(solution)/shard_map/all_gather | solution.py:80
  200.9 5.5 %fusion.94 = (f32[1536]{0:T(1024)S(1)}, f32[1536]{0:T(1024)S(1)}, f32[1536]{0:T(1024)S(1)}, f32[1536]{0:T(1024)S(1)}, f32[1536]{0:T(1024)S(1)}, /*index=5*/f32[1...) fusion(f32[2,158,1536]{2,1,0:T(8,128)S(1)} %maximum_convert_fus, ...), kind=kOutput, calls=%fused_computation.161 | convolution fusion | flops 611037696 | bytes 16594944 | tf_op jit(solution)/shard_map/dot_general | solution.py:78
  206.3 0.6 stack.106
  206.9 2.0 fusion.95
  209.3 0.6 stack.131
  209.9 0.6 stack.132
  210.5 0.6 stack.133
  211.1 0.6 stack.134
  211.7 0.6 stack.135
  212.3 0.6 stack.136
  212.9 1.8 stack.137
  214.7 0.8 broadcast_in_dim.42
  215.5 0.0 all-reduce.2.cloned.1.call-update
  215.5 0.0 reduce-scatter.2.cloned.1.call-start
  215.6 3.6 fusion
  219.2 0.0 reduce-scatter.2.cloned.1.call-update
  219.2 0.6 fusion.142
  219.9 1.9 collective-permute-start.4
  221.8 5.2 %collective-permute-start.3 = (bf16[15,1536]{1,0:T(8,128)(2,1)S(1)}, bf16[15,1536]{1,0:T(8,128)(2,1)S(1)}, u32[]{:S(2)}, u32[]{:S(2)}) collective-permute-start(bf16[15,1536]{1,0:T(8,128)(2,1)S(1)} %get-tuple-element.75), channel_id=1, source_target_pairs={{0,1},{1,2},{2,3},{3,4},{4,5},{5,6},{6,7},{7,8},{8,9},{9,10},{10,1... | collective-permute-start | bytes 138248 | tf_op jit(solution)/shard_map/ppermute | solution.py:21
  227.0 0.0 all-to-all-done
  227.3 0.0 copy-start.62
  227.3 3.9 fusion.10
  231.3 1.9 collective-permute-start.2
  233.2 0.0 collective-permute-done.4
  233.2 0.0 collective-permute-done.3
  233.2 0.1 maximum_convert_fusion.1
  233.7 5.1 %fusion.63 = (f32[1536]{0:T(1024)S(1)}, f32[128]{0:T(128)S(1)}, f32[128]{0:T(128)S(1)}, f32[128,1536]{1,0:T(8,128)S(1)}) fusion(bf16[1,128,1536]{2,1,0:T(8,128)(2,1)S(1)} %copy-done, f32[128]{0:T(128)S(1)} %copy-done.68, f32[128]{0:T(128)S(1)} %copy-done.66, f32[1536]{0:T(1024)S(1)} %reduce.3, f32[128]{0:T(128)S(1)} %copy-done.71, ...), kind=kLoop, calls=%fused_computation.130 | loop fusion | flops 13957376 | bytes 25764352 | tf_op jit(solution)/shard_map/reduce_sum | solution.py:107
  238.8 0.4 fusion.132
  239.2 3.6 collective-permute-start.5
  242.8 31.5 %psum.15 = bf16[1,1536]{1,0:T(2,128)(2,1)S(1)} all-reduce(bf16[1,1536]{1,0:T(2,128)(2,1)S(1)} %broadcast_in_dim.44), channel_id=1, replica_groups=mesh['section'=16,'tm'=16] {'tm'}, use_global_device_ids=true, to_apply=%region_42.43 | all-reduce | flops 1536 | bytes 6144 | tf_op jit(solution)/shard_map/psum | solution.py:110
  274.3 0.6 broadcast_in_dim.45
  274.9 78.6 %all-reduce.2.cloned.1.call-done = bf16[1,31,1536]{2,0,1:T(2,128)(2,1)} async-done(((bf16[1,31,1536]{2,0,1:T(2,128)(2,1)}), bf16[1,31,1536]{2,0,1:T(2,128)(2,1)}) %all-reduce.2.cloned.1.call-update) | async-done | bytes 95248 | tf_op jit(solution)/shard_map/psum | solution.py:109
  353.5 1.8 broadcast_in_dim.43
  355.3 0.0 collective-permute-done.2
  355.3 0.0 collective-permute-done.5
  355.3 111.0 %reduce-scatter.2.cloned.1.call-done = bf16[96,1536]{1,0:T(8,128)(2,1)} async-done(((bf16[1536,1536]{1,0:T(8,128)(2,1)}), bf16[96,1536]{1,0:T(8,128)(2,1)}) %reduce-scatter.2.cloned.1.call-update) | async-done | bytes 294928 | tf_op jit(solution)/shard_map/reduce_scatter | solution.py:119
  466.3 1.8 bitcast_convert_fusion
  468.1 0.7 copy.16
  468.9 0.7 copy.17
  (177 shorter events, 0.5 us)
Async XLA Ops:
  7.2 193.7 %all-gather.3.cloned.1.call-start = ((), (), s32[]{:S(2)}) async-start(), calls=%async_computation.4 | async-start | bytes 5013504 | tf_op jit(solution)/shard_map/all_gather | solution.py:80
  11.5 9.7 %copy-start.69 = (f32[1,1536]{1,0:T(1,128)S(1)}, f32[1,1536]{1,0:T(1,128)}, u32[]{:S(2)}) copy-start(f32[1,1536]{1,0:T(1,128)} %param.11) | copy-start | bytes 18436
  11.5 9.7 %copy-start.72 = (s32[1,2]{1,0:T(1,128)S(1)}, s32[1,2]{1,0:T(1,128)}, u32[]{:S(2)}) copy-start(s32[1,2]{1,0:T(1,128)} %param.15) | copy-start | bytes 28
  11.5 10.3 %copy-start.73 = (s32[32]{0:T(128)S(1)}, s32[32]{0:T(128)}, u32[]{:S(2)}) copy-start(s32[32]{0:T(128)} %param.14) | copy-start | bytes 388
  11.5 13.6 %copy-start = (bf16[1,128,1536]{2,1,0:T(8,128)(2,1)S(1)}, bf16[1,128,1536]{2,1,0:T(8,128)(2,1)}, u32[]{:S(2)}) copy-start(bf16[1,128,1536]{2,1,0:T(8,128)(2,1)} %param.9) | copy-start | bytes 1179652
  11.5 13.7 %copy-start.1 = (bf16[1,128,1536]{2,1,0:T(8,128)(2,1)S(1)}, bf16[1,128,1536]{2,1,0:T(8,128)(2,1)}, u32[]{:S(2)}) copy-start(bf16[1,128,1536]{2,1,0:T(8,128)(2,1)} %param.8) | copy-start | bytes 1179652
  11.5 215.5 %all-to-all-start = ((bf16[16,96,1536]{2,1,0:T(8,128)(2,1)}), bf16[16,96,1536]{2,1,0:T(8,128)(2,1)}, u32[]{:S(2)}, u32[]{:S(2)}) async-start(bf16[16,96,1536]{2,1,0:T(8,128)(2,1)} %stack.105), calls=%async_computation | async-start | bytes 9437184 | tf_op jit(solution)/shard_map/all_to_all | solution.py:11
  21.1 332.4 %all-reduce.2.cloned.1.call-start = ((), (), s32[]{:S(2)}) async-start(), calls=%async_computation.3 | async-start | bytes 380928 | tf_op jit(solution)/shard_map/psum | solution.py:109
  25.6 7.6 %copy-start.4 = (f32[1,31,1536]{2,0,1:T(1,128)S(1)}, f32[1,31,1536]{2,0,1:T(1,128)}, u32[]{:S(2)}) copy-start(f32[1,31,1536]{2,0,1:T(1,128)} %param.12) | copy-start | bytes 571396
  26.4 128.3 %collective-permute-start.1 = (bf16[2,15,1536]{2,1,0:T(8,128)(2,1)S(1)}, bf16[2,15,1536]{2,1,0:T(8,128)(2,1)S(1)}, u32[]{:S(2)}, u32[]{:S(2)}) collective-permute-start(bf16[2,15,1536]{2,1,0:T(8,128)(2,1)S(1)} %get-tuple-element.74), channel_id=1, source_target_pairs={{1,0},{2,1},{3,2},{4,3},{5,4},{6,5},{7,6},{8,7},{9,8},{10,9},{11,1... | collective-permute-start | bytes 276488 | tf_op jit(solution)/shard_map/ppermute | solution.py:22
  28.9 135.2 %collective-permute-start = (bf16[2,15,1536]{2,1,0:T(8,128)(2,1)S(1)}, bf16[2,15,1536]{2,1,0:T(8,128)(2,1)S(1)}, u32[]{:S(2)}, u32[]{:S(2)}) collective-permute-start(bf16[2,15,1536]{2,1,0:T(8,128)(2,1)S(1)} %get-tuple-element.73), channel_id=1, source_target_pairs={{0,1},{1,2},{2,3},{3,4},{4,5},{5,6},{6,7},{7,8},{8,9},{9,10},{10,1... | collective-permute-start | bytes 276488 | tf_op jit(solution)/shard_map/ppermute | solution.py:21
  33.5 130.9 %copy-start.5 = (f32[1536]{0:T(1024)}, f32[1536]{0:T(1024)S(1)}, u32[]{:S(2)}) copy-start(f32[1536]{0:T(1024)S(1)} %get-tuple-element.40) | copy-start | bytes 18436
  33.5 130.9 %copy-start.7 = (f32[1536]{0:T(1024)}, f32[1536]{0:T(1024)S(1)}, u32[]{:S(2)}) copy-start(f32[1536]{0:T(1024)S(1)} %get-tuple-element.41) | copy-start | bytes 18436
  33.5 130.9 %copy-start.9 = (f32[1536]{0:T(1024)}, f32[1536]{0:T(1024)S(1)}, u32[]{:S(2)}) copy-start(f32[1536]{0:T(1024)S(1)} %get-tuple-element.42) | copy-start | bytes 18436
  33.5 130.9 %copy-start.11 = (f32[1536]{0:T(1024)}, f32[1536]{0:T(1024)S(1)}, u32[]{:S(2)}) copy-start(f32[1536]{0:T(1024)S(1)} %get-tuple-element.43) | copy-start | bytes 18436
  33.6 130.9 %copy-start.13 = (f32[1536]{0:T(1024)}, f32[1536]{0:T(1024)S(1)}, u32[]{:S(2)}) copy-start(f32[1536]{0:T(1024)S(1)} %get-tuple-element.44) | copy-start | bytes 18436
  33.6 130.9 %copy-start.15 = (f32[1536]{0:T(1024)}, f32[1536]{0:T(1024)S(1)}, u32[]{:S(2)}) copy-start(f32[1536]{0:T(1024)S(1)} %get-tuple-element.45) | copy-start | bytes 18436
  33.6 130.9 %copy-start.17 = (f32[1536]{0:T(1024)}, f32[1536]{0:T(1024)S(1)}, u32[]{:S(2)}) copy-start(f32[1536]{0:T(1024)S(1)} %get-tuple-element.46) | copy-start | bytes 18436
  33.6 130.9 %copy-start.19 = (f32[1536]{0:T(1024)}, f32[1536]{0:T(1024)S(1)}, u32[]{:S(2)}) copy-start(f32[1536]{0:T(1024)S(1)} %get-tuple-element.47) | copy-start | bytes 18436
  33.6 130.9 %copy-start.21 = (f32[1536]{0:T(1024)}, f32[1536]{0:T(1024)S(1)}, u32[]{:S(2)}) copy-start(f32[1536]{0:T(1024)S(1)} %get-tuple-element.48) | copy-start | bytes 18436
  33.6 130.9 %copy-start.23 = (f32[1536]{0:T(1024)}, f32[1536]{0:T(1024)S(1)}, u32[]{:S(2)}) copy-start(f32[1536]{0:T(1024)S(1)} %get-tuple-element.49) | copy-start | bytes 18436
  33.6 130.9 %copy-start.25 = (f32[1536]{0:T(1024)}, f32[1536]{0:T(1024)S(1)}, u32[]{:S(2)}) copy-start(f32[1536]{0:T(1024)S(1)} %get-tuple-element.50) | copy-start | bytes 18436
  33.6 130.9 %copy-start.27 = (f32[1536]{0:T(1024)}, f32[1536]{0:T(1024)S(1)}, u32[]{:S(2)}) copy-start(f32[1536]{0:T(1024)S(1)} %get-tuple-element.51) | copy-start | bytes 18436
  33.6 130.9 %copy-start.29 = (f32[1536]{0:T(1024)}, f32[1536]{0:T(1024)S(1)}, u32[]{:S(2)}) copy-start(f32[1536]{0:T(1024)S(1)} %get-tuple-element.52) | copy-start | bytes 18436
  33.6 130.9 %copy-start.31 = (f32[1536]{0:T(1024)}, f32[1536]{0:T(1024)S(1)}, u32[]{:S(2)}) copy-start(f32[1536]{0:T(1024)S(1)} %get-tuple-element.53) | copy-start | bytes 18436
  33.7 130.9 %copy-start.33 = (f32[1536]{0:T(1024)}, f32[1536]{0:T(1024)S(1)}, u32[]{:S(2)}) copy-start(f32[1536]{0:T(1024)S(1)} %get-tuple-element.54) | copy-start | bytes 18436
  33.7 130.9 %copy-start.35 = (f32[1536]{0:T(1024)}, f32[1536]{0:T(1024)S(1)}, u32[]{:S(2)}) copy-start(f32[1536]{0:T(1024)S(1)} %get-tuple-element.55) | copy-start | bytes 18436
  33.7 130.9 %copy-start.37 = (f32[1536]{0:T(1024)}, f32[1536]{0:T(1024)S(1)}, u32[]{:S(2)}) copy-start(f32[1536]{0:T(1024)S(1)} %get-tuple-element.56) | copy-start | bytes 18436
  33.7 130.9 %copy-start.39 = (f32[1536]{0:T(1024)}, f32[1536]{0:T(1024)S(1)}, u32[]{:S(2)}) copy-start(f32[1536]{0:T(1024)S(1)} %get-tuple-element.57) | copy-start | bytes 18436
  33.9 137.5 %copy-start.41 = (f32[1536]{0:T(1024)}, f32[1536]{0:T(1024)S(1)}, u32[]{:S(2)}) copy-start(f32[1536]{0:T(1024)S(1)} %get-tuple-element.58) | copy-start | bytes 18436
  33.9 137.5 %copy-start.43 = (f32[1536]{0:T(1024)}, f32[1536]{0:T(1024)S(1)}, u32[]{:S(2)}) copy-start(f32[1536]{0:T(1024)S(1)} %get-tuple-element.59) | copy-start | bytes 18436
  33.9 137.5 %copy-start.45 = (f32[1536]{0:T(1024)}, f32[1536]{0:T(1024)S(1)}, u32[]{:S(2)}) copy-start(f32[1536]{0:T(1024)S(1)} %get-tuple-element.60) | copy-start | bytes 18436
  33.9 137.5 %copy-start.47 = (f32[1536]{0:T(1024)}, f32[1536]{0:T(1024)S(1)}, u32[]{:S(2)}) copy-start(f32[1536]{0:T(1024)S(1)} %get-tuple-element.61) | copy-start | bytes 18436
  33.9 137.5 %copy-start.49 = (f32[1536]{0:T(1024)}, f32[1536]{0:T(1024)S(1)}, u32[]{:S(2)}) copy-start(f32[1536]{0:T(1024)S(1)} %get-tuple-element.62) | copy-start | bytes 18436
  33.9 137.5 %copy-start.51 = (f32[1536]{0:T(1024)}, f32[1536]{0:T(1024)S(1)}, u32[]{:S(2)}) copy-start(f32[1536]{0:T(1024)S(1)} %get-tuple-element.63) | copy-start | bytes 18436
  34.0 137.5 %copy-start.53 = (f32[1536]{0:T(1024)}, f32[1536]{0:T(1024)S(1)}, u32[]{:S(2)}) copy-start(f32[1536]{0:T(1024)S(1)} %get-tuple-element.64) | copy-start | bytes 18436
  34.0 137.5 %copy-start.55 = (f32[1536]{0:T(1024)}, f32[1536]{0:T(1024)S(1)}, u32[]{:S(2)}) copy-start(f32[1536]{0:T(1024)S(1)} %get-tuple-element.65) | copy-start | bytes 18436
  34.0 137.5 %copy-start.57 = (f32[1536]{0:T(1024)}, f32[1536]{0:T(1024)S(1)}, u32[]{:S(2)}) copy-start(f32[1536]{0:T(1024)S(1)} %get-tuple-element.66) | copy-start | bytes 18436
  34.0 137.5 %copy-start.59 = (f32[1536]{0:T(1024)}, f32[1536]{0:T(1024)S(1)}, u32[]{:S(2)}) copy-start(f32[1536]{0:T(1024)S(1)} %get-tuple-element.67) | copy-start | bytes 18436
  34.0 137.5 %copy-start.61 = (f32[1536]{0:T(1024)}, f32[1536]{0:T(1024)S(1)}, u32[]{:S(2)}) copy-start(f32[1536]{0:T(1024)S(1)} %get-tuple-element.68) | copy-start | bytes 18436
  34.0 137.5 %copy-start.63 = (f32[1536]{0:T(1024)}, f32[1536]{0:T(1024)S(1)}, u32[]{:S(2)}) copy-start(f32[1536]{0:T(1024)S(1)} %get-tuple-element.69) | copy-start | bytes 18436
  164.5 36.3 %copy-start.3 = (bf16[1,128,1536]{2,1,0:T(8,128)(2,1)S(1)}, bf16[1,128,1536]{2,1,0:T(8,128)(2,1)}, u32[]{:S(2)}) copy-start(bf16[1,128,1536]{2,1,0:T(8,128)(2,1)} %param.10) | copy-start | bytes 1179652
  208.9 6.6 %copy-start.2 = (f32[2,128,1536]{2,1,0:T(8,128)S(1)}, f32[2,128,1536]{2,1,0:T(8,128)}, u32[]{:S(2)}) copy-start(f32[2,128,1536]{2,1,0:T(8,128)} %fusion.11) | copy-start | bytes 4718596
  215.5 250.8 %reduce-scatter.2.cloned.1.call-start = ((), (), s32[]{:S(2)}) async-start(), calls=%async_computation.2 | async-start | bytes 5013504 | tf_op jit(solution)/shard_map/reduce_scatter | solution.py:119
  219.9 13.3 %collective-permute-start.4 = (bf16[15,1536]{1,0:T(8,128)(2,1)}, bf16[15,1536]{1,0:T(8,128)(2,1)S(1)}, u32[]{:S(2)}, u32[]{:S(2)}) collective-permute-start(bf16[15,1536]{1,0:T(8,128)(2,1)} %get-tuple-element.76), channel_id=1, source_target_pairs={{1,0},{2,1},{3,2},{4,3},{5,4},{6,5},{7,6},{8,7},{9,8},{10,9},{11,1... | collective-permute-start | bytes 138248 | tf_op jit(solution)/shard_map/ppermute | solution.py:22
  221.8 11.4 %collective-permute-start.3 = (bf16[15,1536]{1,0:T(8,128)(2,1)S(1)}, bf16[15,1536]{1,0:T(8,128)(2,1)S(1)}, u32[]{:S(2)}, u32[]{:S(2)}) collective-permute-start(bf16[15,1536]{1,0:T(8,128)(2,1)S(1)} %get-tuple-element.75), channel_id=1, source_target_pairs={{0,1},{1,2},{2,3},{3,4},{4,5},{5,6},{6,7},{7,8},{8,9},{9,10},{10,1... | collective-permute-start | bytes 138248 | tf_op jit(solution)/shard_map/ppermute | solution.py:21
  227.0 6.4 %copy-start.6 = (f32[1536]{0:T(1024)S(1)}, f32[1536]{0:T(1024)}, u32[]{:S(2)}) copy-start(f32[1536]{0:T(1024)} %copy-done.5) | copy-start | bytes 18436
  227.0 6.4 %copy-start.8 = (f32[1536]{0:T(1024)S(1)}, f32[1536]{0:T(1024)}, u32[]{:S(2)}) copy-start(f32[1536]{0:T(1024)} %copy-done.7) | copy-start | bytes 18436
  227.0 6.4 %copy-start.10 = (f32[1536]{0:T(1024)S(1)}, f32[1536]{0:T(1024)}, u32[]{:S(2)}) copy-start(f32[1536]{0:T(1024)} %copy-done.9) | copy-start | bytes 18436
  227.0 6.4 %copy-start.12 = (f32[1536]{0:T(1024)S(1)}, f32[1536]{0:T(1024)}, u32[]{:S(2)}) copy-start(f32[1536]{0:T(1024)} %copy-done.11) | copy-start | bytes 18436
  227.0 6.4 %copy-start.14 = (f32[1536]{0:T(1024)S(1)}, f32[1536]{0:T(1024)}, u32[]{:S(2)}) copy-start(f32[1536]{0:T(1024)} %copy-done.13) | copy-start | bytes 18436
  227.0 6.4 %copy-start.16 = (f32[1536]{0:T(1024)S(1)}, f32[1536]{0:T(1024)}, u32[]{:S(2)}) copy-start(f32[1536]{0:T(1024)} %copy-done.15) | copy-start | bytes 18436
  227.0 6.4 %copy-start.18 = (f32[1536]{0:T(1024)S(1)}, f32[1536]{0:T(1024)}, u32[]{:S(2)}) copy-start(f32[1536]{0:T(1024)} %copy-done.17) | copy-start | bytes 18436
  227.0 6.4 %copy-start.20 = (f32[1536]{0:T(1024)S(1)}, f32[1536]{0:T(1024)}, u32[]{:S(2)}) copy-start(f32[1536]{0:T(1024)} %copy-done.19) | copy-start | bytes 18436
  227.1 6.4 %copy-start.22 = (f32[1536]{0:T(1024)S(1)}, f32[1536]{0:T(1024)}, u32[]{:S(2)}) copy-start(f32[1536]{0:T(1024)} %copy-done.21) | copy-start | bytes 18436
  227.1 6.4 %copy-start.24 = (f32[1536]{0:T(1024)S(1)}, f32[1536]{0:T(1024)}, u32[]{:S(2)}) copy-start(f32[1536]{0:T(1024)} %copy-done.23) | copy-start | bytes 18436
  227.1 6.4 %copy-start.26 = (f32[1536]{0:T(1024)S(1)}, f32[1536]{0:T(1024)}, u32[]{:S(2)}) copy-start(f32[1536]{0:T(1024)} %copy-done.25) | copy-start | bytes 18436
  227.1 6.4 %copy-start.28 = (f32[1536]{0:T(1024)S(1)}, f32[1536]{0:T(1024)}, u32[]{:S(2)}) copy-start(f32[1536]{0:T(1024)} %copy-done.27) | copy-start | bytes 18436
  227.1 6.4 %copy-start.30 = (f32[1536]{0:T(1024)S(1)}, f32[1536]{0:T(1024)}, u32[]{:S(2)}) copy-start(f32[1536]{0:T(1024)} %copy-done.29) | copy-start | bytes 18436
  227.1 6.4 %copy-start.32 = (f32[1536]{0:T(1024)S(1)}, f32[1536]{0:T(1024)}, u32[]{:S(2)}) copy-start(f32[1536]{0:T(1024)} %copy-done.31) | copy-start | bytes 18436
  227.1 6.4 %copy-start.34 = (f32[1536]{0:T(1024)S(1)}, f32[1536]{0:T(1024)}, u32[]{:S(2)}) copy-start(f32[1536]{0:T(1024)} %copy-done.33) | copy-start | bytes 18436
  227.1 6.4 %copy-start.36 = (f32[1536]{0:T(1024)S(1)}, f32[1536]{0:T(1024)}, u32[]{:S(2)}) copy-start(f32[1536]{0:T(1024)} %copy-done.35) | copy-start | bytes 18436
  231.3 124.0 %collective-permute-start.2 = (bf16[1,128,1536]{2,1,0:T(8,128)(2,1)}, bf16[1,128,1536]{2,1,0:T(8,128)(2,1)S(1)}, u32[]{:S(2)}, u32[]{:S(2)}) collective-permute-start(bf16[1,128,1536]{2,1,0:T(8,128)(2,1)} %fusion.10), channel_id=1, source_target_pairs={{0,16},{16,32},{32,48},{48,64},{64,80},{80,96},{96,112},{112,128},... | collective-permute-start | bytes 1179656 | tf_op jit(solution)/shard_map/ppermute | solution.py:30
  239.2 116.1 %collective-permute-start.5 = (bf16[1,128,1536]{2,1,0:T(8,128)(2,1)S(1)}, bf16[1,128,1536]{2,1,0:T(8,128)(2,1)S(1)}, u32[]{:S(2)}, u32[]{:S(2)}) collective-permute-start(bf16[1,128,1536]{2,1,0:T(8,128)(2,1)S(1)} %fusion.132), channel_id=1, source_target_pairs={{16,0},{32,16},{48,32},{64,48},{80,64},{96,80},{112,96},{128,112},... | collective-permute-start | bytes 1179656 | tf_op jit(solution)/shard_map/ppermute | solution.py:30
  (20 other events, 110.8 us)
Sparse Core Ops, SparseCore 0:
  9.8 191.0 all-gather.2
  215.6 137.8 all-reduce.1
  356.1 110.2 reduce-scatter.1
